TPU v7x, 32 devices: a whole 2x2x4 slice. The times are simulated.
32 devices in a mesh: dp: 2 (over y), fsdp: 16 (over z, x, core).
Axes of the slice: x: 2, y: 2, z: 4, core: 2. Of those that a mesh axis runs over, the one named last changes fastest.
Arguments:
- tokens: bfloat16 [65536, 768], P(('dp', 'fsdp')), may hold values from -12 to 12
- cotangent: bfloat16 [65536, 768], P(('dp', 'fsdp')), may hold values from -12 to 12
- segment_ids: int32 [65536], P(('dp', 'fsdp')), may hold values from 0 to 2687, as said below
- first_gain: bfloat16 [768], P('fsdp'), may hold values from 0.25 to 1.75
- first_shift: bfloat16 [768], P('fsdp'), may hold values from -1.75 to 1.75
- triple_weight: bfloat16 [768, 2304], P('fsdp'), may hold values from -0.3125 to 0.3125
- query_bias: bfloat16 [768], P('fsdp'), may hold values from -3 to 3
- value_bias: bfloat16 [768], P('fsdp'), may hold values from -1.75 to 1.75
- out_weight: bfloat16 [768, 768], P('fsdp'), may hold values from -0.875 to 0.875
- out_bias: bfloat16 [768], P('fsdp'), may hold values from -1.75 to 1.75
- second_gain: bfloat16 [768], P('fsdp'), may hold values from 0.25 to 1.75
- second_shift: bfloat16 [768], P('fsdp'), may hold values from -1.75 to 1.75
- up_weight: bfloat16 [768, 3072], P('fsdp'), may hold values from -0.21875 to 0.21875
- up_bias: bfloat16 [3072], P('fsdp'), may hold values from -3 to 3
- down_weight: bfloat16 [3072, 768], P('fsdp'), may hold values from -0.109375 to 0.109375
- down_bias: bfloat16 [768], P('fsdp'), may hold values from -1.75 to 1.75
Outputs:
- block_output: bfloat16 [65536, 768], P(('dp', 'fsdp'))
- tokens_gradient: bfloat16 [65536, 768], P(('dp', 'fsdp'))
- first_gain_gradient: float32 [768], P('fsdp')
- first_shift_gradient: float32 [768], P('fsdp')
- triple_weight_gradient: float32 [768, 2304], P('fsdp')
- query_bias_gradient: float32 [768], P('fsdp')
- value_bias_gradient: float32 [768], P('fsdp')
- out_weight_gradient: float32 [768, 768], P('fsdp')
- out_bias_gradient: float32 [768], P('fsdp')
- second_gain_gradient: float32 [768], P('fsdp')
- second_shift_gradient: float32 [768], P('fsdp')
- up_weight_gradient: float32 [768, 3072], P('fsdp')
- up_bias_gradient: float32 [3072], P('fsdp')
- down_weight_gradient: float32 [3072, 768], P('fsdp')
- down_bias_gradient: float32 [768], P('fsdp')
Inputs may be any that keep to these rules, and one draw needn't show every extreme that they name: `segment_ids`: segment numbers never fall along the patches and no image spans two aligned blocks of 1024 patches; each image has 900 patches and begins its block, or has 1 to 64 patches; the first block begins with an image of 900 patches; the last patch carries exactly the largest number, 65536 // 1024 * (1024 // max(1, 25) + 2) - 1.
All inputs are finite; a program needn't handle non-finite values.
Results may differ from a plain program's by a relative error of at most 0.014.
Values may be sent and summed in bfloat16 or wider, within the bound.
A program may use at most 384 MiB of HBM per device.

v0:
```python
import jax
import jax.numpy as jnp
from jax import lax
from jax.sharding import PartitionSpec as P

H = 12
HD = 64
ROWS = 1024
MB = 2
norm_eps = 1e-06
root_half = 0.7071067811865476
root_inv_two_pi = 0.3989422804014327


def norm_forward(values, gain, shift):
    mean_val = jnp.mean(values, axis=-1, keepdims=True)
    centered = values - mean_val
    variance = jnp.mean(centered * centered, axis=-1, keepdims=True)
    inv_std = lax.rsqrt(variance + norm_eps)
    normed = centered * inv_std
    return (normed * gain + shift, normed, inv_std)


def norm_backward(grad_out, normed, inv_std, gain):
    gain_part = jnp.sum(grad_out * normed, axis=0)
    shift_part = jnp.sum(grad_out, axis=0)
    grad_norm = grad_out * gain
    mean_plain = jnp.mean(grad_norm, axis=-1, keepdims=True)
    mean_cross = jnp.mean(grad_norm * normed, axis=-1, keepdims=True)
    return (inv_std * (grad_norm - mean_plain - normed * mean_cross), gain_part, shift_part)


def gelu_slope(upped):
    normal_cdf = 0.5 * (1.0 + lax.erf(upped * root_half))
    return normal_cdf + upped * jnp.exp(-0.5 * upped * upped) * root_inv_two_pi


def masked_scores(query_block, keys, seg_block, segments):
    scores = (
        jnp.einsum("qhd,khd->hqk", query_block, keys, preferred_element_type=jnp.float32) * 0.125
    )
    allowed = seg_block[:, None] == segments[None, :]
    return jnp.where(allowed[None], scores, -1e30)


def attend_forward(query, keys, value, segments):
    row_count = query.shape[0]
    block = min(512, row_count)
    pieces = []
    log_totals = []
    for begin in range(0, row_count, block):
        scores = masked_scores(
            query[begin : begin + block], keys, segments[begin : begin + block], segments
        )
        peak = jnp.max(scores, axis=-1, keepdims=True)
        exponent = jnp.exp(scores - peak)
        total = jnp.sum(exponent, axis=-1, keepdims=True)
        soft_low = (exponent / total).astype(jnp.bfloat16)
        pieces.append(
            jnp.einsum("hqk,khd->qhd", soft_low, value, preferred_element_type=jnp.float32)
        )
        log_totals.append(peak[..., 0] + jnp.log(total[..., 0]))
    return (jnp.concatenate(pieces, axis=0), jnp.concatenate(log_totals, axis=1))


def attend_backward(query, keys, value, segments, log_total, grad_mixed):
    row_count = query.shape[0]
    block = min(512, row_count)
    query_grads = []
    key_grad = jnp.zeros(keys.shape, jnp.float32)
    value_grad = jnp.zeros(value.shape, jnp.float32)
    for begin in range(0, row_count, block):
        query_block = query[begin : begin + block]
        grad_block = grad_mixed[begin : begin + block]
        scores = masked_scores(query_block, keys, segments[begin : begin + block], segments)
        soft = jnp.exp(scores - log_total[:, begin : begin + block, None])
        grad_soft = jnp.einsum(
            "qhd,khd->hqk", grad_block, value, preferred_element_type=jnp.float32
        )
        center = jnp.sum(soft * grad_soft, axis=-1, keepdims=True)
        grad_scores = (soft * (grad_soft - center)).astype(jnp.bfloat16)
        query_grads.append(
            jnp.einsum("hqk,khd->qhd", grad_scores, keys, preferred_element_type=jnp.float32)
            * 0.125
        )
        key_grad = (
            key_grad
            + jnp.einsum(
                "hqk,qhd->khd", grad_scores, query_block, preferred_element_type=jnp.float32
            )
            * 0.125
        )
        value_grad = value_grad + jnp.einsum(
            "hqk,qhd->khd",
            soft.astype(jnp.bfloat16),
            grad_block,
            preferred_element_type=jnp.float32,
        )
    return (jnp.concatenate(query_grads, axis=0), key_grad, value_grad)


def layer_forward(full, inputs, segments):
    (
        first_gain,
        first_shift,
        triple_weight,
        query_bias,
        value_bias,
        out_weight,
        out_bias,
        second_gain,
        second_shift,
        up_weight,
        up_bias,
        down_weight,
        down_bias,
    ) = full
    width = out_weight.shape[0]
    values = inputs.astype(jnp.float32)
    first_h, first_n, first_r = norm_forward(
        values, first_gain.astype(jnp.float32), first_shift.astype(jnp.float32)
    )
    first_in = first_h.astype(jnp.bfloat16)
    projected = jnp.dot(first_in, triple_weight, preferred_element_type=jnp.float32)
    query = (
        (projected[:, :width] + query_bias.astype(jnp.float32))
        .astype(jnp.bfloat16)
        .reshape(-1, H, HD)
    )
    keys = projected[:, width : 2 * width].astype(jnp.bfloat16).reshape(-1, H, HD)
    value = (
        (projected[:, 2 * width :] + value_bias.astype(jnp.float32))
        .astype(jnp.bfloat16)
        .reshape(-1, H, HD)
    )
    attended, log_total = attend_forward(query, keys, value, segments)
    mixed = attended.reshape(-1, width).astype(jnp.bfloat16)
    resid = (
        values
        + jnp.dot(mixed, out_weight, preferred_element_type=jnp.float32)
        + out_bias.astype(jnp.float32)
    )
    second_h, second_n, second_r = norm_forward(
        resid, second_gain.astype(jnp.float32), second_shift.astype(jnp.float32)
    )
    second_in = second_h.astype(jnp.bfloat16)
    upped = jnp.dot(second_in, up_weight, preferred_element_type=jnp.float32) + up_bias.astype(
        jnp.float32
    )
    act = jax.nn.gelu(upped, approximate=False).astype(jnp.bfloat16)
    result = (
        resid
        + jnp.dot(act, down_weight, preferred_element_type=jnp.float32)
        + down_bias.astype(jnp.float32)
    )
    saved = (
        first_n,
        first_r,
        first_in,
        query,
        keys,
        value,
        log_total,
        mixed,
        second_n,
        second_r,
        second_in,
        upped,
        act,
    )
    return (result.astype(jnp.bfloat16), saved)


def layer_backward(full, saved, grad_result, segments):
    (
        first_gain,
        first_shift,
        triple_weight,
        query_bias,
        value_bias,
        out_weight,
        out_bias,
        second_gain,
        second_shift,
        up_weight,
        up_bias,
        down_weight,
        down_bias,
    ) = full
    (
        first_n,
        first_r,
        first_in,
        query,
        keys,
        value,
        log_total,
        mixed,
        second_n,
        second_r,
        second_in,
        upped,
        act,
    ) = saved
    width = out_weight.shape[0]
    grad_out = grad_result.astype(jnp.float32)
    down_bias_part = jnp.sum(grad_out, axis=0)
    grad_low = grad_out.astype(jnp.bfloat16)
    down_weight_part = jnp.einsum("rf,rd->fd", act, grad_low, preferred_element_type=jnp.float32)
    grad_act = jnp.einsum("rd,fd->rf", grad_low, down_weight, preferred_element_type=jnp.float32)
    grad_up = grad_act * gelu_slope(upped)
    up_bias_part = jnp.sum(grad_up, axis=0)
    grad_up_low = grad_up.astype(jnp.bfloat16)
    up_weight_part = jnp.einsum(
        "rd,rf->df", second_in, grad_up_low, preferred_element_type=jnp.float32
    )
    grad_second = jnp.einsum(
        "rf,df->rd", grad_up_low, up_weight, preferred_element_type=jnp.float32
    )
    resid_part, second_gain_part, second_shift_part = norm_backward(
        grad_second, second_n, second_r, second_gain.astype(jnp.float32)
    )
    grad_resid = grad_out + resid_part
    out_bias_part = jnp.sum(grad_resid, axis=0)
    resid_low = grad_resid.astype(jnp.bfloat16)
    out_weight_part = jnp.einsum("rd,re->de", mixed, resid_low, preferred_element_type=jnp.float32)
    grad_mixed = jnp.einsum(
        "re,de->rd", resid_low, out_weight, preferred_element_type=jnp.float32
    ).astype(jnp.bfloat16)
    query_grad, key_grad, value_grad = attend_backward(
        query, keys, value, segments, log_total, grad_mixed.reshape(-1, H, HD)
    )
    query_low = query_grad.reshape(-1, width).astype(jnp.bfloat16)
    key_low = key_grad.reshape(-1, width).astype(jnp.bfloat16)
    value_low = value_grad.reshape(-1, width).astype(jnp.bfloat16)
    query_bias_part = jnp.sum(query_low, axis=0, dtype=jnp.float32)
    value_bias_part = jnp.sum(value_low, axis=0, dtype=jnp.float32)
    grad_projected = jnp.concatenate([query_low, key_low, value_low], axis=1)
    triple_weight_part = jnp.einsum(
        "rd,re->de", first_in, grad_projected, preferred_element_type=jnp.float32
    )
    grad_first = jnp.einsum(
        "re,de->rd", grad_projected, triple_weight, preferred_element_type=jnp.float32
    )
    input_part, first_gain_part, first_shift_part = norm_backward(
        grad_first, first_n, first_r, first_gain.astype(jnp.float32)
    )
    grad_inputs = (grad_resid + input_part).astype(jnp.bfloat16)
    parts = (
        first_gain_part,
        first_shift_part,
        triple_weight_part,
        query_bias_part,
        value_bias_part,
        out_weight_part,
        out_bias_part,
        second_gain_part,
        second_shift_part,
        up_weight_part,
        up_bias_part,
        down_weight_part,
        down_bias_part,
    )
    return (grad_inputs, parts)


def on_device(
    tokens,
    cotangent,
    segment_ids,
    first_gain,
    first_shift,
    triple_weight,
    query_bias,
    value_bias,
    out_weight,
    out_bias,
    second_gain,
    second_shift,
    up_weight,
    up_bias,
    down_weight,
    down_bias,
):
    shards = (
        first_gain,
        first_shift,
        triple_weight,
        query_bias,
        value_bias,
        out_weight,
        out_bias,
        second_gain,
        second_shift,
        up_weight,
        up_bias,
        down_weight,
        down_bias,
    )
    totals = tuple((jnp.zeros(piece.shape, jnp.float32) for piece in shards))
    results = []
    input_grads = []
    for micro in range(MB):
        lower = micro * ROWS
        segments = segment_ids[lower : lower + ROWS]
        forward_full = (
            lax.all_gather(first_gain, "fsdp", axis=0, tiled=True),
            lax.all_gather(first_shift, "fsdp", axis=0, tiled=True),
            lax.all_gather(triple_weight, "fsdp", axis=0, tiled=True),
            lax.all_gather(query_bias, "fsdp", axis=0, tiled=True),
            lax.all_gather(value_bias, "fsdp", axis=0, tiled=True),
            lax.all_gather(out_weight, "fsdp", axis=0, tiled=True),
            lax.all_gather(out_bias, "fsdp", axis=0, tiled=True),
            lax.all_gather(second_gain, "fsdp", axis=0, tiled=True),
            lax.all_gather(second_shift, "fsdp", axis=0, tiled=True),
            lax.all_gather(up_weight, "fsdp", axis=0, tiled=True),
            lax.all_gather(up_bias, "fsdp", axis=0, tiled=True),
            lax.all_gather(down_weight, "fsdp", axis=0, tiled=True),
            lax.all_gather(down_bias, "fsdp", axis=0, tiled=True),
        )
        result, saved = layer_forward(forward_full, tokens[lower : lower + ROWS], segments)
        results.append(result)
        backward_full = (
            lax.all_gather(first_gain, "fsdp", axis=0, tiled=True),
            lax.all_gather(first_shift, "fsdp", axis=0, tiled=True),
            lax.all_gather(triple_weight, "fsdp", axis=0, tiled=True),
            lax.all_gather(query_bias, "fsdp", axis=0, tiled=True),
            lax.all_gather(value_bias, "fsdp", axis=0, tiled=True),
            lax.all_gather(out_weight, "fsdp", axis=0, tiled=True),
            lax.all_gather(out_bias, "fsdp", axis=0, tiled=True),
            lax.all_gather(second_gain, "fsdp", axis=0, tiled=True),
            lax.all_gather(second_shift, "fsdp", axis=0, tiled=True),
            lax.all_gather(up_weight, "fsdp", axis=0, tiled=True),
            lax.all_gather(up_bias, "fsdp", axis=0, tiled=True),
            lax.all_gather(down_weight, "fsdp", axis=0, tiled=True),
            lax.all_gather(down_bias, "fsdp", axis=0, tiled=True),
        )
        grad_inputs, parts = layer_backward(
            backward_full, saved, cotangent[lower : lower + ROWS], segments
        )
        input_grads.append(grad_inputs)
        p0, p1, p2, p3, p4, p5, p6, p7, p8, p9, p10, p11, p12 = parts
        summed = (
            lax.psum_scatter(p0, "fsdp", scatter_dimension=0, tiled=True),
            lax.psum_scatter(p1, "fsdp", scatter_dimension=0, tiled=True),
            lax.psum_scatter(p2, "fsdp", scatter_dimension=0, tiled=True),
            lax.psum_scatter(p3, "fsdp", scatter_dimension=0, tiled=True),
            lax.psum_scatter(p4, "fsdp", scatter_dimension=0, tiled=True),
            lax.psum_scatter(p5, "fsdp", scatter_dimension=0, tiled=True),
            lax.psum_scatter(p6, "fsdp", scatter_dimension=0, tiled=True),
            lax.psum_scatter(p7, "fsdp", scatter_dimension=0, tiled=True),
            lax.psum_scatter(p8, "fsdp", scatter_dimension=0, tiled=True),
            lax.psum_scatter(p9, "fsdp", scatter_dimension=0, tiled=True),
            lax.psum_scatter(p10, "fsdp", scatter_dimension=0, tiled=True),
            lax.psum_scatter(p11, "fsdp", scatter_dimension=0, tiled=True),
            lax.psum_scatter(p12, "fsdp", scatter_dimension=0, tiled=True),
        )
        totals = tuple((left + right for left, right in zip(totals, summed)))
    s0, s1, s2, s3, s4, s5, s6, s7, s8, s9, s10, s11, s12 = totals
    final = (
        lax.psum(s0.astype(jnp.bfloat16), "dp").astype(jnp.float32),
        lax.psum(s1.astype(jnp.bfloat16), "dp").astype(jnp.float32),
        lax.psum(s2.astype(jnp.bfloat16), "dp").astype(jnp.float32),
        lax.psum(s3.astype(jnp.bfloat16), "dp").astype(jnp.float32),
        lax.psum(s4.astype(jnp.bfloat16), "dp").astype(jnp.float32),
        lax.psum(s5.astype(jnp.bfloat16), "dp").astype(jnp.float32),
        lax.psum(s6.astype(jnp.bfloat16), "dp").astype(jnp.float32),
        lax.psum(s7.astype(jnp.bfloat16), "dp").astype(jnp.float32),
        lax.psum(s8.astype(jnp.bfloat16), "dp").astype(jnp.float32),
        lax.psum(s9.astype(jnp.bfloat16), "dp").astype(jnp.float32),
        lax.psum(s10.astype(jnp.bfloat16), "dp").astype(jnp.float32),
        lax.psum(s11.astype(jnp.bfloat16), "dp").astype(jnp.float32),
        lax.psum(s12.astype(jnp.bfloat16), "dp").astype(jnp.float32),
    )
    return (
        jnp.concatenate(results, axis=0),
        jnp.concatenate(input_grads, axis=0),
        final[0],
        final[1],
        final[2],
        final[3],
        final[4],
        final[5],
        final[6],
        final[7],
        final[8],
        final[9],
        final[10],
        final[11],
        final[12],
    )


def solution(mesh):
    in_specs = (
        P(("dp", "fsdp"), None),
        P(("dp", "fsdp"), None),
        P(("dp", "fsdp")),
        P("fsdp"),
        P("fsdp"),
        P("fsdp", None),
        P("fsdp"),
        P("fsdp"),
        P("fsdp", None),
        P("fsdp"),
        P("fsdp"),
        P("fsdp"),
        P("fsdp", None),
        P("fsdp"),
        P("fsdp", None),
        P("fsdp"),
    )
    out_specs = (
        P(("dp", "fsdp"), None),
        P(("dp", "fsdp"), None),
        P("fsdp"),
        P("fsdp"),
        P("fsdp", None),
        P("fsdp"),
        P("fsdp"),
        P("fsdp", None),
        P("fsdp"),
        P("fsdp"),
        P("fsdp"),
        P("fsdp", None),
        P("fsdp"),
        P("fsdp", None),
        P("fsdp"),
    )
    return jax.shard_map(
        on_device, mesh=mesh, in_specs=in_specs, out_specs=out_specs, check_vma=False
    )
```

profile of v0, /device:TPU:0, one launch (start us, length us, event | category | flops | bytes accessed | tf_op | source)
XLA Modules:
  0.0 1104.1 jit_solution(5142248432136446658)
XLA Ops:
  21.7 63.5 %all-reduce.19 = (bf16[768]{0:T(1024)(128)(2,1)S(1)}, bf16[768]{0:T(1024)(128)(2,1)S(1)}, bf16[768]{0:T(1024)(128)(2,1)S(1)}, bf16[768]{0:T(1024)(128)(2,1)S(1)}...) all-reduce(bf16[768]{0:T(1024)(128)(2,1)S(1)} %dynamic-update-slice, ...), channel_id=1, replica_groups=mesh['dp'=2,'fsdp'=16] {'fsdp'}, use_global_device_ids=true, to_apply=%add.1 | all-reduce | flops 9216 | bytes 36864
  144.8 12.3 %fusion.55 = (f32[12,512]{1,0:T(8,128)S(1)}, f32[12,512,1024]{2,1,0:T(8,128)}) fusion(pred[512,1024]{1,0:T(8,128)(4,1)} %get-tuple-element.151, bf16[512,12,64]{0,2,1:T(8,128)(2,1)} %bitcast.134, bf16[1024,12,64]{0,2,1:T(8,128)(2,1)S(1)} %bitcast.116), kind=kOutput, calls=%fused_computation.95 | convolution fusion | flops 824174592 | bytes 28073984 | tf_op jit(solution)/shard_map/qhd,khd->hqk/dot_general | solution.py:40
  157.1 12.5 %fusion.1 = f32[12,512]{1,0:T(8,128)S(1)} fusion(f32[12,512]{1,0:T(8,128)S(1)} %get-tuple-element.122, f32[12,512,1024]{2,1,0:T(8,128)} %get-tuple-element.123, pred[512,1024]{1,0:T(8,128)(4,1)} %get-tuple-element.151), kind=kLoop, calls=%fused_computation.25 | loop fusion | flops 25159680 | bytes 25739264 | tf_op jit(solution)/shard_map/reduce_sum | solution.py:57
  182.8 12.1 %fusion.54 = (f32[12,512]{1,0:T(8,128)S(1)}, f32[12,512,1024]{2,1,0:T(8,128)}) fusion(pred[512,1024]{1,0:T(8,128)(4,1)} %get-tuple-element.152, bf16[512,12,64]{0,2,1:T(8,128)(2,1)} %bitcast.136, bf16[1024,12,64]{0,2,1:T(8,128)(2,1)S(1)} %bitcast.117), kind=kOutput, calls=%fused_computation.94 | convolution fusion | flops 824174592 | bytes 28073984 | tf_op jit(solution)/shard_map/qhd,khd->hqk/dot_general | solution.py:40
  194.9 13.6 %fusion = f32[12,512]{1,0:T(8,128)S(1)} fusion(f32[12,512]{1,0:T(8,128)S(1)} %get-tuple-element.124, f32[12,512,1024]{2,1,0:T(8,128)} %get-tuple-element.125, pred[512,1024]{1,0:T(8,128)(4,1)} %get-tuple-element.152), kind=kLoop, calls=%fused_computation.24 | loop fusion | flops 25159680 | bytes 25739264 | tf_op jit(solution)/shard_map/reduce_sum | solution.py:57
  219.8 12.3 %fusion.57 = (f32[12,512]{1,0:T(8,128)S(1)}, f32[12,512,1024]{2,1,0:T(8,128)}) fusion(pred[512,1024]{1,0:T(8,128)(4,1)S(1)} %copy-done.29, bf16[512,12,64]{0,2,1:T(8,128)(2,1)} %bitcast.132, bf16[1024,12,64]{0,2,1:T(8,128)(2,1)S(1)} %bitcast.120), kind=kOutput, calls=%fused_computation.97 | convolution fusion | flops 824174592 | bytes 28073984 | tf_op jit(solution)/shard_map/qhd,khd->hqk/dot_general | solution.py:40
  232.1 12.3 %fusion.3 = f32[12,512]{1,0:T(8,128)S(1)} fusion(f32[12,512]{1,0:T(8,128)S(1)} %get-tuple-element.118, f32[12,512,1024]{2,1,0:T(8,128)} %get-tuple-element.119, pred[512,1024]{1,0:T(8,128)(4,1)S(1)} %copy-done.29), kind=kLoop, calls=%fused_computation.27 | loop fusion | flops 25159680 | bytes 25739264 | tf_op jit(solution)/shard_map/reduce_sum | solution.py:57
  255.9 12.0 %fusion.56 = (f32[12,512]{1,0:T(8,128)S(1)}, f32[12,512,1024]{2,1,0:T(8,128)}) fusion(pred[512,1024]{1,0:T(8,128)(4,1)S(1)} %copy-done.26, bf16[512,12,64]{0,2,1:T(8,128)(2,1)} %bitcast.138, bf16[1024,12,64]{0,2,1:T(8,128)(2,1)S(1)} %bitcast.121), kind=kOutput, calls=%fused_computation.96 | convolution fusion | flops 824174592 | bytes 28073984 | tf_op jit(solution)/shard_map/qhd,khd->hqk/dot_general | solution.py:40
  268.0 12.3 %fusion.2 = f32[12,512]{1,0:T(8,128)S(1)} fusion(f32[12,512]{1,0:T(8,128)S(1)} %get-tuple-element.120, f32[12,512,1024]{2,1,0:T(8,128)} %get-tuple-element.121, pred[512,1024]{1,0:T(8,128)(4,1)S(1)} %copy-done.26), kind=kLoop, calls=%fused_computation.26 | loop fusion | flops 25159680 | bytes 25739264 | tf_op jit(solution)/shard_map/reduce_sum | solution.py:57
  304.6 11.0 fusion.153
  315.6 13.5 %fusion.166 = (f32[3072]{0:T(1024)}, bf16[1024,3072]{1,0:T(8,128)(2,1)S(1)}) fusion(f32[1024,3072]{1,0:T(8,128)} %fusion.153, f32[3072]{0:T(1024)S(1)} %copy-done.99, bf16[3072,768]{1,0:T(8,128)(2,1)} %all-gather.11.cloned.1.call-done, bf16[2048,768]{1,0:T(8,128)(2,1)} %param.17), kind=kOutput, calls=%fused_computation.289 | convolution fusion | flops 4869583872 | bytes 25190400 | tf_op jit(solution)/shard_map/rd,fd->rf/dot_general | solution.py:210
  335.8 61.5 %fusion.10 = (bf16[1024,3072]{1,0:T(8,128)(2,1)}, bf16[1024,3072]{1,0:T(8,128)(2,1)}, f32[1024,3072]{1,0:T(8,128)}) fusion(f32[3072]{0:T(1024)S(1)} %copy-done.99, f32[1024,3072]{1,0:T(8,128)S(1)} %bitcast.165, bf16[768,3072]{1,0:T(8,128)(2,1)S(1)} %copy-done.110, f32[1024,768]{1,0:T(8,128)S(1)} %get-tuple-element.127, f32[768]{0:T(1024)S(1)} %copy-done.64, ...), kind=kOutput, calls=%fused_computation.38 | convolution fusion | flops 5251006464 | bytes 45639680 | tf_op jit(solution)/shard_map/dot_general | solution.py:147
  397.4 12.0 %fusion.165 = (f32[3072]{0:T(1024)}, bf16[1024,3072]{1,0:T(8,128)(2,1)S(1)}) fusion(f32[1024,3072]{1,0:T(8,128)} %get-tuple-element.130, f32[3072]{0:T(1024)S(1)} %copy-done.99, bf16[3072,768]{1,0:T(8,128)(2,1)} %all-gather.11.cloned.1.call-done, bf16[2048,768]{1,0:T(8,128)(2,1)S(1)} %copy-done.48), kind=kOutput, calls=%fused_computation.288 | convolution fusion | flops 4869583872 | bytes 25190400 | tf_op jit(solution)/shard_map/rd,fd->rf/dot_general | solution.py:210
  409.4 12.9 %multiply_reduce_fusion.5 = (f32[768]{0:T(1024)}, f32[1024]{0:T(1024)S(1)}, f32[1024]{0:T(1024)S(1)}, f32[768]{0:T(1024)}, f32[768]{0:T(1024)}, /*index=5*/f32[1...) fusion(f32[1024,768]{1,0:T(8,128)S(1)} %get-tuple-element.127, f32[1024]{0:T(1024)S(1)} %add_rsqrt_fusion.2, ...), kind=kOutput, calls=%fused_computation.160 | convolution fusion | flops 4845985792 | bytes 23641088 | tf_op jit(solution)/shard_map/rf,df->rd/dot_general | solution.py:217
  431.6 21.7 %multiply_reduce_fusion.1 = (f32[12,512]{1,0:T(8,128)S(1)}, f32[12,512,1024]{2,1,0:T(8,128)}) fusion(f32[12,512]{1,0:T(8,128)S(1)} %copy-done.71, f32[12,512,1024]{2,1,0:T(8,128)} %get-tuple-element.121, pred[512,1024]{1,0:T(8,128)(4,1)S(1)} %copy-done.27, bf16[512,12,64]{0,2,1:T(8,128)(2,1)S(1)} %bitcast.146, bf16[1024,12,64]{0,2,1:T(8,128)(2,1)S(1)} %bitcast.130), kind=kOutput, calls=%fused_computation.4 | convolution fusion | flops 836757504 | bytes 53264384 | tf_op jit(solution)/shard_map/qhd,khd->hqk/dot_general | solution.py:77
  453.3 17.4 %multiply_convert_fusion.1 = bf16[12,512,1024]{2,1,0:T(8,128)(2,1)S(1)} fusion(f32[12,512,1024]{2,1,0:T(8,128)} %get-tuple-element.137, f32[12,512]{1,0:T(8,128)S(1)} %get-tuple-element.136, f32[12,512]{1,0:T(8,128)S(1)} %copy-done.71, f32[12,512,1024]{2,1,0:T(8,128)} %get-tuple-element.121, pred[512,1024]{1,0:T(8,128)(4,1)} %get-tuple-element.114), kind=kLoop, calls=%fused_computation.3 | loop fusion | flops 37748736 | bytes 63488000 | tf_op jit(solution)/shard_map/convert_element_type | solution.py:81
  482.2 13.2 %fusion.24 = f32[12,64,1024]{2,1,0:T(8,128)} fusion(bf16[512,12,64]{0,2,1:T(8,128)(2,1)S(1)} %bitcast.150, f32[12,512]{1,0:T(8,128)S(1)} %copy-done.74, f32[12,512,1024]{2,1,0:T(8,128)} %get-tuple-element.119, pred[512,1024]{1,0:T(8,128)(4,1)S(1)} %copy-done.30), kind=kOutput, calls=%fused_computation.52 | convolution fusion | flops 830472192 | bytes 29646848 | tf_op jit(solution)/shard_map/hqk,qhd->khd/dot_general | solution.py:93
  495.4 21.8 %multiply_reduce_fusion = (f32[12,512]{1,0:T(8,128)S(1)}, f32[12,512,1024]{2,1,0:T(8,128)}) fusion(f32[12,512]{1,0:T(8,128)S(1)} %copy-done.74, f32[12,512,1024]{2,1,0:T(8,128)} %get-tuple-element.119, pred[512,1024]{1,0:T(8,128)(4,1)S(1)} %copy-done.31, bf16[512,12,64]{0,2,1:T(8,128)(2,1)S(1)} %bitcast.151, bf16[1024,12,64]{0,2,1:T(8,128)(2,1)S(1)} %bitcast.131), kind=kOutput, calls=%fused_computation.1 | convolution fusion | flops 836757504 | bytes 53264384 | tf_op jit(solution)/shard_map/qhd,khd->hqk/dot_general | solution.py:77
  525.0 21.6 %multiply_reduce_fusion.3 = (f32[12,512]{1,0:T(8,128)S(1)}, f32[12,512,1024]{2,1,0:T(8,128)}) fusion(f32[12,512]{1,0:T(8,128)S(1)} %copy-done.75, f32[12,512,1024]{2,1,0:T(8,128)} %get-tuple-element.125, pred[512,1024]{1,0:T(8,128)(4,1)S(1)} %copy-done.33, bf16[512,12,64]{0,2,1:T(8,128)(2,1)S(1)} %bitcast.148, bf16[1024,12,64]{0,2,1:T(8,128)(2,1)S(1)} %bitcast.127), kind=kOutput, calls=%fused_computation.10 | convolution fusion | flops 836757504 | bytes 53264384 | tf_op jit(solution)/shard_map/qhd,khd->hqk/dot_general | solution.py:77
  546.6 17.2 %multiply_convert_fusion.3 = bf16[12,512,1024]{2,1,0:T(8,128)(2,1)S(1)} fusion(f32[12,512,1024]{2,1,0:T(8,128)} %get-tuple-element.133, f32[12,512]{1,0:T(8,128)S(1)} %get-tuple-element.132, f32[12,512]{1,0:T(8,128)S(1)} %copy-done.75, f32[12,512,1024]{2,1,0:T(8,128)} %get-tuple-element.125, pred[512,1024]{1,0:T(8,128)(4,1)} %get-tuple-element.152), kind=kLoop, calls=%fused_computation.9 | loop fusion | flops 37748736 | bytes 63488000 | tf_op jit(solution)/shard_map/convert_element_type | solution.py:81
  575.3 13.3 %fusion.28 = f32[12,64,1024]{2,1,0:T(8,128)} fusion(bf16[512,12,64]{0,2,1:T(8,128)(2,1)S(1)} %bitcast.153, f32[12,512]{1,0:T(8,128)S(1)} %copy-done.73, f32[12,512,1024]{2,1,0:T(8,128)} %get-tuple-element.123, pred[512,1024]{1,0:T(8,128)(4,1)S(1)} %copy-done.28), kind=kOutput, calls=%fused_computation.54 | convolution fusion | flops 830472192 | bytes 29646848 | tf_op jit(solution)/shard_map/hqk,qhd->khd/dot_general | solution.py:93
  588.5 18.4 %multiply_reduce_fusion.2 = (f32[12,512]{1,0:T(8,128)S(1)}, f32[12,512,1024]{2,1,0:T(8,128)}) fusion(f32[12,512]{1,0:T(8,128)S(1)} %copy-done.73, f32[12,512,1024]{2,1,0:T(8,128)} %get-tuple-element.123, pred[512,1024]{1,0:T(8,128)(4,1)} %get-tuple-element.151, bf16[512,12,64]{0,2,1:T(8,128)(2,1)} %bitcast.152, bf16[1024,12,64]{0,2,1:T(8,128)(2,1)} %bitcast.124), kind=kOutput, calls=%fused_computation.7 | convolution fusion | flops 836757504 | bytes 53264384 | tf_op jit(solution)/shard_map/qhd,khd->hqk/dot_general | solution.py:77
  611.9 15.1 %convert_reduce_fusion.5 = (f32[12,64]{1,0:T(8,128)S(1)}, bf16[12,64,1024]{2,1,0:T(8,128)(2,1)}) fusion(f32[12,64,1024]{2,1,0:T(8,128)} %fusion.28, bf16[512,12,64]{0,2,1:T(8,128)(2,1)} %bitcast.149, f32[12,512]{1,0:T(8,128)S(1)} %copy-done.75, f32[12,512,1024]{2,1,0:T(8,128)} %get-tuple-element.125, pred[512,1024]{1,0:T(8,128)(4,1)} %get-tuple-element.152), kind=kOutput, calls=%fused_computation.162 | convolution fusion | flops 833617152 | bytes 31222784 | tf_op jit(solution)/shard_map/hqk,qhd->khd/dot_general | solution.py:93
  627.0 17.6 %multiply_convert_fusion = bf16[12,512,1024]{2,1,0:T(8,128)(2,1)S(1)} fusion(f32[12,512,1024]{2,1,0:T(8,128)} %get-tuple-element.139, f32[12,512]{1,0:T(8,128)S(1)} %get-tuple-element.138, f32[12,512]{1,0:T(8,128)S(1)} %copy-done.74, f32[12,512,1024]{2,1,0:T(8,128)} %get-tuple-element.119, pred[512,1024]{1,0:T(8,128)(4,1)} %get-tuple-element.115), kind=kLoop, calls=%fused_computation | loop fusion | flops 37748736 | bytes 63488000 | tf_op jit(solution)/shard_map/convert_element_type | solution.py:81
  650.9 22.7 %multiply_convert_fusion.2 = bf16[12,512,1024]{2,1,0:T(8,128)(2,1)} fusion(f32[12,512,1024]{2,1,0:T(8,128)} %get-tuple-element.135, f32[12,512]{1,0:T(8,128)S(1)} %get-tuple-element.134, f32[12,512]{1,0:T(8,128)S(1)} %copy-done.73, f32[12,512,1024]{2,1,0:T(8,128)} %get-tuple-element.123, pred[512,1024]{1,0:T(8,128)(4,1)} %get-tuple-element.151), kind=kLoop, calls=%fused_computation.6 | loop fusion | flops 37748736 | bytes 63488000 | tf_op jit(solution)/shard_map/convert_element_type | solution.py:81
  706.5 13.3 %convert_reduce_fusion.4 = (f32[12,64]{1,0:T(8,128)S(1)}, bf16[12,64,1024]{2,1,0:T(8,128)(2,1)S(1)}) fusion(f32[12,64,1024]{2,1,0:T(8,128)} %fusion.24, bf16[512,12,64]{0,2,1:T(8,128)(2,1)} %bitcast.147, f32[12,512]{1,0:T(8,128)S(1)} %copy-done.72, f32[12,512,1024]{2,1,0:T(8,128)} %get-tuple-element.121, pred[512,1024]{1,0:T(8,128)(4,1)} %get-tuple-element.114), kind=kOutput, calls=%fused_computation.161 | convolution fusion | flops 833617152 | bytes 31222784 | tf_op jit(solution)/shard_map/hqk,qhd->khd/dot_general | solution.py:93
  741.8 11.6 %convolution_add_fusion.2 = f32[768,3072]{1,0:T(8,128)} fusion(f32[768,3072]{1,0:T(8,128)S(1)} %fusion.97, bf16[1024,3072]{1,0:T(8,128)(2,1)} %copy-done.40, f32[1024,768]{1,0:T(8,128)S(1)} %copy-done.16, f32[1024]{0:T(1024)S(1)} %copy-done.82, f32[1024]{0:T(1024)S(1)} %copy-done.70, f32[768]{0:T(1024)S(1)} %copy-done.65, f32[768]{0:T(1024)S(1)} %copy-done.63), kind=kOutput, calls=%fused_computation.100 | convolution fusion | flops 4838129664 | bytes 28325888 | tf_op jit(solution)/shard_map/rd,rf->df/dot_general | solution.py:214
  761.4 10.5 convolution_add_fusion.1
  789.2 58.9 %all-reduce.18 = (bf16[768]{0:T(1024)(128)(2,1)S(1)}, bf16[768]{0:T(1024)(128)(2,1)S(1)}, bf16[768]{0:T(1024)(128)(2,1)S(1)}, bf16[768]{0:T(1024)(128)(2,1)S(1)}...) all-reduce(f32[768]{0:T(1024)S(1)} %add.387, ...), channel_id=15, replica_groups=mesh['dp'=2,'fsdp'=16] {'fsdp'}, use_global_device_ids=true, to_apply=%region_29.30.clone | all-reduce | flops 9216 | bytes 55296
  881.2 52.8 %reduce-scatter.9.cloned.1.call-done = f32[48,3072]{1,0:T(8,128)} async-done(((f32[768,3072]{1,0:T(8,128)}), f32[48,3072]{1,0:T(8,128)}) %reduce-scatter.9.cloned.1.call-update) | async-done | bytes 589840 | tf_op jit(solution)/shard_map/reduce_scatter | solution.py:353
  935.7 114.0 %reduce-scatter.11.cloned.1.call-done = f32[192,768]{1,0:T(8,128)} async-done(((f32[3072,768]{1,0:T(8,128)}), f32[192,768]{1,0:T(8,128)}) %reduce-scatter.11.cloned.1.call-update) | async-done | bytes 589840 | tf_op jit(solution)/shard_map/reduce_scatter | solution.py:355
  1059.4 30.7 %all-reduce.24.cloned.1.call-done = (bf16[48,2304]{1,0:T(8,128)(2,1)}, bf16[48,768]{1,0:T(8,128)(2,1)}, bf16[48,3072]{1,0:T(8,128)(2,1)}, bf16[192,768]{1,0:T(8,128)(2,1)}) async-done(((bf16[48,2304]{1,0:T(8,128)(2,1)}, bf16[48,768]{1,0:T(8,128)(2,1)}, bf16[48,3072]{1,0:T(8,128)(2,1)}, bf16[192,768]{1,0:T(8,128)(2,1)}), (bf16[48,2304]{1,0:T(8,128)(2,1)}, bf16[48,768]{1,0:T(8,128)(2,1)}, ...) | async-done | bytes 884752 | tf_op jit(solution)/shard_map/psum | solution.py:363
  (411 shorter events, 320.1 us)
Async XLA Ops:
  7.2 82.3 %copy-start.8 = (bf16[2048,768]{1,0:T(8,128)(2,1)S(1)}, bf16[2048,768]{1,0:T(8,128)(2,1)}, u32[]{:S(2)}) copy-start(bf16[2048,768]{1,0:T(8,128)(2,1)} %param.16) | copy-start | bytes 9437188
  7.2 86.4 %all-gather.5.cloned.1.call-start = ((), (), s32[]{:S(2)}) async-start(), calls=%async_computation.4 | async-start | bytes 3760128 | tf_op jit(solution)/shard_map/all_gather | solution.py:309
  7.9 285.6 %all-gather.7.cloned.1.call-start = ((), (), s32[]{:S(2)}) async-start(), calls=%async_computation.5 | async-start | bytes 1253376 | tf_op jit(solution)/shard_map/all_gather | solution.py:312
  8.7 295.9 %all-gather.9.cloned.1.call-start = ((), (), s32[]{:S(2)}) async-start(), calls=%async_computation.6 | async-start | bytes 5013504 | tf_op jit(solution)/shard_map/all_gather | solution.py:316
  9.4 306.1 %all-gather.11.cloned.1.call-start = ((), (), s32[]{:S(2)}) async-start(), calls=%async_computation.7 | async-start | bytes 5013504 | tf_op jit(solution)/shard_map/all_gather | solution.py:318
  10.0 867.7 %reduce-scatter.7.cloned.1.call-start = ((), (), s32[]{:S(2)}) async-start(), calls=%async_computation.9 | async-start | bytes 2506752 | tf_op jit(solution)/shard_map/reduce_scatter | solution.py:349
  85.2 19.1 %copy-start.106 = (f32[768]{0:T(1024)}, f32[768]{0:T(1024)S(1)}, u32[]{:S(2)}) copy-start(f32[768]{0:T(1024)S(1)} %convert_element_type.312) | copy-start | bytes 9220
  85.2 19.1 %copy-start.93 = (f32[768]{0:T(1024)}, f32[768]{0:T(1024)S(1)}, u32[]{:S(2)}) copy-start(f32[768]{0:T(1024)S(1)} %convert_element_type.311) | copy-start | bytes 9220
  104.3 151.6 %copy-start.5 = (bf16[1024,768]{0,1:T(8,128)(2,1)}, bf16[1024,768]{0,1:T(8,128)(2,1)S(1)}, u32[]{:S(2)}) copy-start(bf16[1024,768]{0,1:T(8,128)(2,1)S(1)} %copy.69) | copy-start | bytes 4718596
  118.2 64.6 %copy-start.4 = (bf16[1024,768]{0,1:T(8,128)(2,1)}, bf16[1024,768]{0,1:T(8,128)(2,1)S(1)}, u32[]{:S(2)}) copy-start(bf16[1024,768]{0,1:T(8,128)(2,1)S(1)} %copy.65) | copy-start | bytes 4718596
  144.8 24.9 %copy-start.21 = (bf16[1024,768]{0,1:T(8,128)(2,1)S(1)}, bf16[1024,768]{0,1:T(8,128)(2,1)}, u32[]{:S(2)}) copy-start(bf16[1024,768]{0,1:T(8,128)(2,1)} %copy.63) | copy-start | bytes 4718596
  157.1 16.2 %copy-start.1 = (f32[12,512,1024]{2,1,0:T(8,128)S(1)}, f32[12,512,1024]{2,1,0:T(8,128)}, u32[]{:S(2)}) copy-start(f32[12,512,1024]{2,1,0:T(8,128)} %get-tuple-element.123) | copy-start | bytes 75497472
  194.9 16.3 %copy-start.3 = (f32[12,512,1024]{2,1,0:T(8,128)S(1)}, f32[12,512,1024]{2,1,0:T(8,128)}, u32[]{:S(2)}) copy-start(f32[12,512,1024]{2,1,0:T(8,128)} %get-tuple-element.125) | copy-start | bytes 75497472
  194.9 16.4 %copy-start.32 = (pred[512,1024]{1,0:T(8,128)(4,1)S(1)}, pred[512,1024]{1,0:T(8,128)(4,1)}, u32[]{:S(2)}) copy-start(pred[512,1024]{1,0:T(8,128)(4,1)} %get-tuple-element.152) | copy-start | bytes 1572868
  219.7 24.6 %copy-start.23 = (bf16[1024,768]{0,1:T(8,128)(2,1)S(1)}, bf16[1024,768]{0,1:T(8,128)(2,1)}, u32[]{:S(2)}) copy-start(bf16[1024,768]{0,1:T(8,128)(2,1)} %copy.67) | copy-start | bytes 4718596
  255.9 24.4 %copy-start.60 = (bf16[512,12,64]{0,2,1:T(8,128)(2,1)S(1)}, bf16[512,12,64]{0,2,1:T(8,128)(2,1)}, u32[]{:S(2)}) copy-start(bf16[512,12,64]{0,2,1:T(8,128)(2,1)} %fusion.113) | copy-start | bytes 2359300
  268.0 16.1 %copy-start = (f32[12,512,1024]{2,1,0:T(8,128)S(1)}, f32[12,512,1024]{2,1,0:T(8,128)}, u32[]{:S(2)}) copy-start(f32[12,512,1024]{2,1,0:T(8,128)} %get-tuple-element.121) | copy-start | bytes 75497472
  297.5 124.8 %copy-start.6 = (f32[1024,768]{1,0:T(8,128)}, f32[1024,768]{1,0:T(8,128)S(1)}, u32[]{:S(2)}) copy-start(f32[1024,768]{1,0:T(8,128)S(1)} %get-tuple-element.127) | copy-start | bytes 9437188
  297.6 124.8 %copy-start.66 = (f32[1024]{0:T(1024)}, f32[1024]{0:T(1024)S(1)}, u32[]{:S(2)}) copy-start(f32[1024]{0:T(1024)S(1)} %broadcast_multiply_fusion.10) | copy-start | bytes 12292
  298.1 124.3 %copy-start.78 = (f32[1024]{0:T(1024)}, f32[1024]{0:T(1024)S(1)}, u32[]{:S(2)}) copy-start(f32[1024]{0:T(1024)S(1)} %add_rsqrt_fusion.2) | copy-start | bytes 12292
  299.8 15.7 %copy-start.68 = (f32[1024]{0:T(1024)}, f32[1024]{0:T(1024)S(1)}, u32[]{:S(2)}) copy-start(f32[1024]{0:T(1024)S(1)} %broadcast_multiply_fusion.8) | copy-start | bytes 12292
  315.6 20.2 %slice-start = ((s8[12582912]{0:T(1024)(128)(4,1)}), s8[4194304]{0:T(1024)(128)(4,1)S(1)}, s32[]{:S(2)}) async-start(s8[12582912]{0:T(1024)(128)(4,1)} %bitcast.164), calls=%async_computation.13 | async-start | bytes 8388608
  315.6 20.2 %slice-start.1 = ((s8[12582912]{0:T(1024)(128)(4,1)}), s8[4194304]{0:T(1024)(128)(4,1)S(1)}, s32[]{:S(2)}) async-start(s8[12582912]{0:T(1024)(128)(4,1)} %bitcast.164), calls=%async_computation.14 | async-start | bytes 8388608
  335.8 61.6 %copy-start.48 = (bf16[2048,768]{1,0:T(8,128)(2,1)S(1)}, bf16[2048,768]{1,0:T(8,128)(2,1)}, u32[]{:S(2)}) copy-start(bf16[2048,768]{1,0:T(8,128)(2,1)} %param.17) | copy-start | bytes 9437188
  431.6 21.7 %copy-start.52 = (bf16[512,768]{0,1:T(8,128)(2,1)}, bf16[512,768]{0,1:T(8,128)(2,1)S(1)}, u32[]{:S(2)}) copy-start(bf16[512,768]{0,1:T(8,128)(2,1)S(1)} %get-tuple-element.92) | copy-start | bytes 2359300
  525.0 21.6 %copy-start.53 = (bf16[512,768]{0,1:T(8,128)(2,1)}, bf16[512,768]{0,1:T(8,128)(2,1)S(1)}, u32[]{:S(2)}) copy-start(bf16[512,768]{0,1:T(8,128)(2,1)S(1)} %get-tuple-element.90) | copy-start | bytes 2359300
  588.5 18.4 %copy-start.19 = (f32[1024,768]{1,0:T(8,128)S(1)}, f32[1024,768]{1,0:T(8,128)}, u32[]{:S(2)}) copy-start(f32[1024,768]{1,0:T(8,128)} %copy-done.18) | copy-start | bytes 9437188
  611.9 267.6 %reduce-scatter.5.cloned.1.call-start = ((), (), s32[]{:S(2)}) async-start(), calls=%async_computation.8 | async-start | bytes 7520256 | tf_op jit(solution)/shard_map/reduce_scatter | solution.py:346
  731.3 202.6 %reduce-scatter.9.cloned.1.call-start = ((), (), s32[]{:S(2)}) async-start(), calls=%async_computation.10 | async-start | bytes 10027008 | tf_op jit(solution)/shard_map/reduce_scatter | solution.py:353
  753.5 296.2 %reduce-scatter.11.cloned.1.call-start = ((), (), s32[]{:S(2)}) async-start(), calls=%async_computation.11 | async-start | bytes 10027008 | tf_op jit(solution)/shard_map/reduce_scatter | solution.py:355
  772.1 318.1 %all-reduce.24.cloned.1.call-start = ((), (), s32[]{:S(2)}) async-start(), calls=%async_computation.12 | async-start | bytes 1769472 | tf_op jit(solution)/shard_map/psum | solution.py:363
  875.8 175.8 %copy-start.13 = (bf16[2048,768]{1,0:T(8,128)(2,1)S(1)}, bf16[2048,768]{1,0:T(8,128)(2,1)}, u32[]{:S(2)}) copy-start(bf16[2048,768]{1,0:T(8,128)(2,1)} %param.16) | copy-start | bytes 9437188
  (98 other events, 672.5 us)
Sparse Core Ops, SparseCore 0:
  10.3 49.9 all-gather.4
  62.6 37.2 all-gather.6
  102.2 52.1 all-gather.8
  156.5 51.7 all-gather.10
  612.0 60.1 reduce-scatter.6
  731.4 87.4 reduce-scatter.4
  823.0 110.8 reduce-scatter.8
  938.6 111.0 reduce-scatter.10
  1053.3 36.7 all-reduce.23
where the time goes:
time: 1120 us; the launch traced here: 1100 us
  matrix products  511 us (46%)
  waiting for transfers between devices  200 us (18%)
  other arithmetic  186 us (17%)
  blocking collectives  127 us (11%)
  local copies, waits for them, and re-layouts  60.9 us (5%)
  between operations  18.3 us (2%)
    unnamed x2, blocking collectives  122 us
    reduce_scatter x1, waiting for transfers between devices, on_device(): lax.psum_scatter(p11, 'fsdp', scatter_dimension=0, tiled=True)  114 us
    dot_general x4, matrix products, attend_backward(): jnp.einsum('qhd,khd->hqk', grad_block, value, preferred_element_type=jnp....  83.5 us
    convert_element_type x4, other arithmetic, attend_backward(): grad_scores = (soft * (grad_soft - center)).astype(jnp.bfloat16)  74.9 us
    dot_general x2, matrix products, layer_forward(): jnp.dot(second_in, up_weight, preferred_element_type=jnp.float32)  72.5 us
    dot_general x4, matrix products, attend_backward(): jnp.einsum('hqk,qhd->khd', soft.astype(jnp.bfloat16), grad_block, preferr...  54.9 us
    reduce_scatter x1, waiting for transfers between devices, on_device(): lax.psum_scatter(p9, 'fsdp', scatter_dimension=0, tiled=True)  52.8 us
    reduce_sum x4, other arithmetic, attend_forward(): total = jnp.sum(exponent, axis=-1, keepdims=True)  50.7 us
  transfers between devices with their start and end apart: 9, of which 3 were waited for; matrix products, arithmetic and copies ran while one was open for 39% of the time, Pallas kernels for 0%

commit v1 on v0

--- a/solution.py
+++ b/solution.py
@@ -360,7 +360,7 @@
     final = (
         lax.psum(s0.astype(jnp.bfloat16), "dp").astype(jnp.float32),
         lax.psum(s1.astype(jnp.bfloat16), "dp").astype(jnp.float32),
-        lax.psum(s2.astype(jnp.bfloat16), "dp").astype(jnp.float32),
+        jnp.sum(lax.all_gather(s2.astype(jnp.bfloat16), "dp"), axis=0).astype(jnp.float32),
         lax.psum(s3.astype(jnp.bfloat16), "dp").astype(jnp.float32),
         lax.psum(s4.astype(jnp.bfloat16), "dp").astype(jnp.float32),
         lax.psum(s5.astype(jnp.bfloat16), "dp").astype(jnp.float32),

time: 1120 us -> 946 us (0.84)
  waiting for transfers between devices: 200 us -> 19 us
    reduce_scatter x1, waiting for transfers between devices: 114 us -> 0.01 us  [on_device(): lax.psum_scatter(p11, 'fsdp', scatter_dimension=0, tiled=True)]
    reduce_scatter x1, waiting for transfers between devices: 52.8 us -> 0.01 us  [on_device(): lax.psum_scatter(p9, 'fsdp', scatter_dimension=0, tiled=True)]
    psum x1, waiting for transfers between devices: 30.7 us -> 16.3 us  [on_device(): lax.psum(s5.astype(jnp.bfloat16), 'dp').astype(jnp.float32)]
    unnamed x270 -> x278, local copies, waits for them, and re-layouts: 34.5 us -> 35.7 us
  transfers between devices with their start and end apart: 9 -> 9, of which waited for: 3 -> 1; matrix products, arithmetic and copies ran while one was open for 39% -> 65% of each run, Pallas kernels for 0% -> 0%
where the time goes in v1:
time: 946 us; the launch traced here: 935 us
  matrix products  504 us (53%)
  other arithmetic  191 us (20%)
  blocking collectives  138 us (15%)
  local copies, waits for them, and re-layouts  62.6 us (7%)
  waiting for transfers between devices  19 us (2%)
  between operations  18.4 us (2%)
    unnamed x2, blocking collectives  123 us
    dot_general x4, matrix products, attend_backward(): jnp.einsum('qhd,khd->hqk', grad_block, value, preferred_element_type=jnp....  86.8 us
    convert_element_type x4, other arithmetic, attend_backward(): grad_scores = (soft * (grad_soft - center)).astype(jnp.bfloat16)  76.7 us
    dot_general x2, matrix products, layer_forward(): jnp.dot(second_in, up_weight, preferred_element_type=jnp.float32)  72.6 us
    reduce_sum x4, other arithmetic, attend_forward(): total = jnp.sum(exponent, axis=-1, keepdims=True)  50.7 us
    dot_general x4, matrix products, masked_scores(): jnp.einsum('qhd,khd->hqk', query_block, keys, preferred_element_type=jnp....  48.8 us
    dot_general x4, matrix products, attend_backward(): jnp.einsum('hqk,qhd->khd', soft.astype(jnp.bfloat16), grad_block, preferr...  47.4 us
    unnamed x278, local copies, waits for them, and re-layouts  35.7 us
  transfers between devices with their start and end apart: 9, of which 1 were waited for; matrix products, arithmetic and copies ran while one was open for 65% of the time, Pallas kernels for 0%

profile of v1, /device:TPU:0, one launch (start us, length us, event | category | flops | bytes accessed | tf_op | source)
XLA Modules:
  0.0 934.5 jit_solution(5794656785630088483)
XLA Ops:
  21.7 63.5 %all-reduce.19 = (bf16[768]{0:T(1024)(128)(2,1)S(1)}, bf16[768]{0:T(1024)(128)(2,1)S(1)}, bf16[768]{0:T(1024)(128)(2,1)S(1)}, bf16[768]{0:T(1024)(128)(2,1)S(1)}...) all-reduce(bf16[768]{0:T(1024)(128)(2,1)S(1)} %dynamic-update-slice, ...), channel_id=1, replica_groups=mesh['dp'=2,'fsdp'=16] {'fsdp'}, use_global_device_ids=true, to_apply=%add.1 | all-reduce | flops 9216 | bytes 36864
  144.7 12.3 %fusion.55 = (f32[12,512]{1,0:T(8,128)S(1)}, f32[12,512,1024]{2,1,0:T(8,128)}) fusion(pred[512,1024]{1,0:T(8,128)(4,1)} %get-tuple-element.150, bf16[512,12,64]{0,2,1:T(8,128)(2,1)} %bitcast.137, bf16[1024,12,64]{0,2,1:T(8,128)(2,1)S(1)} %bitcast.119), kind=kOutput, calls=%fused_computation.95 | convolution fusion | flops 824174592 | bytes 28073984 | tf_op jit(solution)/shard_map/qhd,khd->hqk/dot_general | solution.py:40
  157.0 12.5 %fusion.1 = f32[12,512]{1,0:T(8,128)S(1)} fusion(f32[12,512]{1,0:T(8,128)S(1)} %get-tuple-element.121, f32[12,512,1024]{2,1,0:T(8,128)} %get-tuple-element.122, pred[512,1024]{1,0:T(8,128)(4,1)} %get-tuple-element.150), kind=kLoop, calls=%fused_computation.25 | loop fusion | flops 25159680 | bytes 25739264 | tf_op jit(solution)/shard_map/reduce_sum | solution.py:57
  182.7 12.2 %fusion.54 = (f32[12,512]{1,0:T(8,128)S(1)}, f32[12,512,1024]{2,1,0:T(8,128)}) fusion(pred[512,1024]{1,0:T(8,128)(4,1)} %get-tuple-element.151, bf16[512,12,64]{0,2,1:T(8,128)(2,1)} %bitcast.141, bf16[1024,12,64]{0,2,1:T(8,128)(2,1)S(1)} %bitcast.120), kind=kOutput, calls=%fused_computation.94 | convolution fusion | flops 824174592 | bytes 28073984 | tf_op jit(solution)/shard_map/qhd,khd->hqk/dot_general | solution.py:40
  194.9 13.6 %fusion = f32[12,512]{1,0:T(8,128)S(1)} fusion(f32[12,512]{1,0:T(8,128)S(1)} %get-tuple-element.123, f32[12,512,1024]{2,1,0:T(8,128)} %get-tuple-element.124, pred[512,1024]{1,0:T(8,128)(4,1)} %get-tuple-element.151), kind=kLoop, calls=%fused_computation.24 | loop fusion | flops 25159680 | bytes 25739264 | tf_op jit(solution)/shard_map/reduce_sum | solution.py:57
  219.8 12.2 %fusion.57 = (f32[12,512]{1,0:T(8,128)S(1)}, f32[12,512,1024]{2,1,0:T(8,128)}) fusion(pred[512,1024]{1,0:T(8,128)(4,1)S(1)} %copy-done.25, bf16[512,12,64]{0,2,1:T(8,128)(2,1)} %bitcast.135, bf16[1024,12,64]{0,2,1:T(8,128)(2,1)S(1)} %bitcast.123), kind=kOutput, calls=%fused_computation.97 | convolution fusion | flops 824174592 | bytes 28073984 | tf_op jit(solution)/shard_map/qhd,khd->hqk/dot_general | solution.py:40
  232.0 12.3 %fusion.3 = f32[12,512]{1,0:T(8,128)S(1)} fusion(f32[12,512]{1,0:T(8,128)S(1)} %get-tuple-element.117, f32[12,512,1024]{2,1,0:T(8,128)} %get-tuple-element.118, pred[512,1024]{1,0:T(8,128)(4,1)S(1)} %copy-done.25), kind=kLoop, calls=%fused_computation.27 | loop fusion | flops 25159680 | bytes 25739264 | tf_op jit(solution)/shard_map/reduce_sum | solution.py:57
  255.9 12.1 %fusion.56 = (f32[12,512]{1,0:T(8,128)S(1)}, f32[12,512,1024]{2,1,0:T(8,128)}) fusion(pred[512,1024]{1,0:T(8,128)(4,1)S(1)} %copy-done.22, bf16[512,12,64]{0,2,1:T(8,128)(2,1)} %bitcast.139, bf16[1024,12,64]{0,2,1:T(8,128)(2,1)S(1)} %bitcast.124), kind=kOutput, calls=%fused_computation.96 | convolution fusion | flops 824174592 | bytes 28073984 | tf_op jit(solution)/shard_map/qhd,khd->hqk/dot_general | solution.py:40
  267.9 12.3 %fusion.2 = f32[12,512]{1,0:T(8,128)S(1)} fusion(f32[12,512]{1,0:T(8,128)S(1)} %get-tuple-element.119, f32[12,512,1024]{2,1,0:T(8,128)} %get-tuple-element.120, pred[512,1024]{1,0:T(8,128)(4,1)S(1)} %copy-done.22), kind=kLoop, calls=%fused_computation.26 | loop fusion | flops 25159680 | bytes 25739264 | tf_op jit(solution)/shard_map/reduce_sum | solution.py:57
  304.5 11.0 %fusion.153 = f32[1024,3072]{1,0:T(8,128)} fusion(bf16[768,3072]{1,0:T(8,128)(2,1)} %all-gather.10.cloned.1.call-done, f32[1024,768]{1,0:T(8,128)} %copy-done.13, f32[1024]{0:T(1024)S(1)} %add_rsqrt_fusion, f32[1024]{0:T(1024)S(1)} %broadcast_multiply_fusion.8, f32[768]{0:T(1024)S(1)} %copy-done.66, f32[768]{0:T(1024)S(1)} %copy-done.65), kind=kOutput, calls=%fused_computation.276 | convolution fusion | flops 4835770368 | bytes 20461568 | tf_op jit(solution)/shard_map/dot_general | solution.py:147
  315.6 13.5 %fusion.166 = (f32[3072]{0:T(1024)}, bf16[1024,3072]{1,0:T(8,128)(2,1)S(1)}) fusion(f32[1024,3072]{1,0:T(8,128)} %fusion.153, f32[3072]{0:T(1024)S(1)} %copy-done.95, bf16[3072,768]{1,0:T(8,128)(2,1)} %all-gather.12.cloned.1.call-done, bf16[2048,768]{1,0:T(8,128)(2,1)} %param.17), kind=kOutput, calls=%fused_computation.289 | convolution fusion | flops 4869583872 | bytes 25190400 | tf_op jit(solution)/shard_map/rd,fd->rf/dot_general | solution.py:210
  335.9 61.6 %fusion.10 = (bf16[1024,3072]{1,0:T(8,128)(2,1)}, bf16[1024,3072]{1,0:T(8,128)(2,1)}, f32[1024,3072]{1,0:T(8,128)}) fusion(f32[3072]{0:T(1024)S(1)} %copy-done.95, f32[1024,3072]{1,0:T(8,128)S(1)} %bitcast.173, bf16[768,3072]{1,0:T(8,128)(2,1)S(1)} %copy-done.106, f32[1024,768]{1,0:T(8,128)S(1)} %get-tuple-element.126, f32[768]{0:T(1024)S(1)} %copy-done.66, ...), kind=kOutput, calls=%fused_computation.38 | convolution fusion | flops 5251006464 | bytes 45639680 | tf_op jit(solution)/shard_map/dot_general | solution.py:147
  397.5 12.0 %fusion.165 = (f32[3072]{0:T(1024)}, bf16[1024,3072]{1,0:T(8,128)(2,1)S(1)}) fusion(f32[1024,3072]{1,0:T(8,128)} %get-tuple-element.129, f32[3072]{0:T(1024)S(1)} %copy-done.95, bf16[3072,768]{1,0:T(8,128)(2,1)} %all-gather.12.cloned.1.call-done, bf16[2048,768]{1,0:T(8,128)(2,1)S(1)} %copy-done.48), kind=kOutput, calls=%fused_computation.288 | convolution fusion | flops 4869583872 | bytes 25190400 | tf_op jit(solution)/shard_map/rd,fd->rf/dot_general | solution.py:210
  409.5 12.9 %multiply_reduce_fusion.5 = (f32[768]{0:T(1024)}, f32[1024]{0:T(1024)S(1)}, f32[1024]{0:T(1024)S(1)}, f32[768]{0:T(1024)}, f32[768]{0:T(1024)}, /*index=5*/f32[1...) fusion(f32[1024,768]{1,0:T(8,128)S(1)} %get-tuple-element.126, f32[1024]{0:T(1024)S(1)} %add_rsqrt_fusion.2, ...), kind=kOutput, calls=%fused_computation.160 | convolution fusion | flops 4845985792 | bytes 23641088 | tf_op jit(solution)/shard_map/rf,df->rd/dot_general | solution.py:217
  447.1 11.3 %convolution_add_fusion.2 = f32[768,3072]{1,0:T(8,128)} fusion(f32[768,3072]{1,0:T(8,128)S(1)} %fusion.97, bf16[1024,3072]{1,0:T(8,128)(2,1)} %copy-done.40, f32[1024,768]{1,0:T(8,128)S(1)} %copy-done.15, f32[1024]{0:T(1024)S(1)} %copy-done.78, f32[1024]{0:T(1024)S(1)} %copy-done.68, f32[768]{0:T(1024)S(1)} %copy-done.66, f32[768]{0:T(1024)S(1)} %copy-done.65), kind=kOutput, calls=%fused_computation.100 | convolution fusion | flops 4838129664 | bytes 28325888 | tf_op jit(solution)/shard_map/rd,rf->df/dot_general | solution.py:214
  460.2 21.5 %multiply_reduce_fusion.1 = (f32[12,512]{1,0:T(8,128)S(1)}, f32[12,512,1024]{2,1,0:T(8,128)}) fusion(f32[12,512]{1,0:T(8,128)S(1)} %copy-done.69, f32[12,512,1024]{2,1,0:T(8,128)} %get-tuple-element.120, pred[512,1024]{1,0:T(8,128)(4,1)S(1)} %copy-done.23, bf16[512,12,64]{0,2,1:T(8,128)(2,1)S(1)} %bitcast.151, bf16[1024,12,64]{0,2,1:T(8,128)(2,1)S(1)} %bitcast.134), kind=kOutput, calls=%fused_computation.4 | convolution fusion | flops 836757504 | bytes 53264384 | tf_op jit(solution)/shard_map/qhd,khd->hqk/dot_general | solution.py:77
  481.8 17.3 %multiply_convert_fusion.1 = bf16[12,512,1024]{2,1,0:T(8,128)(2,1)S(1)} fusion(f32[12,512,1024]{2,1,0:T(8,128)} %get-tuple-element.136, f32[12,512]{1,0:T(8,128)S(1)} %get-tuple-element.135, f32[12,512]{1,0:T(8,128)S(1)} %copy-done.69, f32[12,512,1024]{2,1,0:T(8,128)} %get-tuple-element.120, pred[512,1024]{1,0:T(8,128)(4,1)} %get-tuple-element.113), kind=kLoop, calls=%fused_computation.3 | loop fusion | flops 37748736 | bytes 63488000 | tf_op jit(solution)/shard_map/convert_element_type | solution.py:81
  506.6 20.6 %multiply_reduce_fusion = (f32[12,512]{1,0:T(8,128)S(1)}, f32[12,512,1024]{2,1,0:T(8,128)}) fusion(f32[12,512]{1,0:T(8,128)S(1)} %copy-done.71, f32[12,512,1024]{2,1,0:T(8,128)} %get-tuple-element.118, pred[512,1024]{1,0:T(8,128)(4,1)} %get-tuple-element.114, bf16[512,12,64]{0,2,1:T(8,128)(2,1)} %bitcast.153, bf16[1024,12,64]{0,2,1:T(8,128)(2,1)} %bitcast.131), kind=kOutput, calls=%fused_computation.1 | convolution fusion | flops 836757504 | bytes 53264384 | tf_op jit(solution)/shard_map/qhd,khd->hqk/dot_general | solution.py:77
  527.2 18.3 %multiply_convert_fusion = bf16[12,512,1024]{2,1,0:T(8,128)(2,1)S(1)} fusion(f32[12,512,1024]{2,1,0:T(8,128)} %get-tuple-element.138, f32[12,512]{1,0:T(8,128)S(1)} %get-tuple-element.137, f32[12,512]{1,0:T(8,128)S(1)} %copy-done.71, f32[12,512,1024]{2,1,0:T(8,128)} %get-tuple-element.118, pred[512,1024]{1,0:T(8,128)(4,1)} %get-tuple-element.114), kind=kLoop, calls=%fused_computation | loop fusion | flops 37748736 | bytes 63488000 | tf_op jit(solution)/shard_map/convert_element_type | solution.py:81
  561.4 10.6 %convolution_add_fusion.1 = f32[3072,768]{1,0:T(8,128)} fusion(f32[3072,768]{1,0:T(8,128)S(1)} %fusion.118, bf16[1024,3072]{1,0:T(8,128)(2,1)} %get-tuple-element.98, bf16[2048,768]{1,0:T(8,128)(2,1)S(1)} %copy-done.49), kind=kOutput, calls=%fused_computation.99 | convolution fusion | flops 4834197504 | bytes 26738688 | tf_op jit(solution)/shard_map/rf,rd->fd/dot_general | solution.py:209
  573.8 21.7 %multiply_reduce_fusion.3 = (f32[12,512]{1,0:T(8,128)S(1)}, f32[12,512,1024]{2,1,0:T(8,128)}) fusion(f32[12,512]{1,0:T(8,128)S(1)} %copy-done.73, f32[12,512,1024]{2,1,0:T(8,128)} %get-tuple-element.124, pred[512,1024]{1,0:T(8,128)(4,1)S(1)} %copy-done.28, bf16[512,12,64]{0,2,1:T(8,128)(2,1)S(1)} %bitcast.155, bf16[1024,12,64]{0,2,1:T(8,128)(2,1)S(1)} %bitcast.129), kind=kOutput, calls=%fused_computation.10 | convolution fusion | flops 836757504 | bytes 53264384 | tf_op jit(solution)/shard_map/qhd,khd->hqk/dot_general | solution.py:77
  595.5 22.1 %multiply_convert_fusion.3 = bf16[12,512,1024]{2,1,0:T(8,128)(2,1)} fusion(f32[12,512,1024]{2,1,0:T(8,128)} %get-tuple-element.132, f32[12,512]{1,0:T(8,128)S(1)} %get-tuple-element.131, f32[12,512]{1,0:T(8,128)S(1)} %copy-done.73, f32[12,512,1024]{2,1,0:T(8,128)} %get-tuple-element.124, pred[512,1024]{1,0:T(8,128)(4,1)S(1)} %copy-done.28), kind=kLoop, calls=%fused_computation.9 | loop fusion | flops 37748736 | bytes 63488000 | tf_op jit(solution)/shard_map/convert_element_type | solution.py:81
  617.6 22.9 %multiply_reduce_fusion.2 = (f32[12,512]{1,0:T(8,128)S(1)}, f32[12,512,1024]{2,1,0:T(8,128)}) fusion(f32[12,512]{1,0:T(8,128)S(1)} %copy-done.74, f32[12,512,1024]{2,1,0:T(8,128)} %get-tuple-element.122, pred[512,1024]{1,0:T(8,128)(4,1)S(1)} %copy-done.30, bf16[512,12,64]{0,2,1:T(8,128)(2,1)S(1)} %bitcast.157, bf16[1024,12,64]{0,2,1:T(8,128)(2,1)S(1)} %bitcast.130), kind=kOutput, calls=%fused_computation.7 | convolution fusion | flops 836757504 | bytes 53264384 | tf_op jit(solution)/shard_map/qhd,khd->hqk/dot_general | solution.py:77
  640.5 19.0 %multiply_convert_fusion.2 = bf16[12,512,1024]{2,1,0:T(8,128)(2,1)S(1)} fusion(f32[12,512,1024]{2,1,0:T(8,128)} %get-tuple-element.134, f32[12,512]{1,0:T(8,128)S(1)} %get-tuple-element.133, f32[12,512]{1,0:T(8,128)S(1)} %copy-done.74, f32[12,512,1024]{2,1,0:T(8,128)} %get-tuple-element.122, pred[512,1024]{1,0:T(8,128)(4,1)} %get-tuple-element.150), kind=kLoop, calls=%fused_computation.6 | loop fusion | flops 37748736 | bytes 63488000 | tf_op jit(solution)/shard_map/convert_element_type | solution.py:81
  704.2 11.5 %fusion.28 = f32[12,64,1024]{2,1,0:T(8,128)S(1)} fusion(bf16[512,12,64]{0,2,1:T(8,128)(2,1)S(1)} %bitcast.158, f32[12,512]{1,0:T(8,128)S(1)} %copy-done.74, f32[12,512,1024]{2,1,0:T(8,128)} %get-tuple-element.122, pred[512,1024]{1,0:T(8,128)(4,1)S(1)} %copy-done.31), kind=kOutput, calls=%fused_computation.54 | convolution fusion | flops 830472192 | bytes 29646848 | tf_op jit(solution)/shard_map/hqk,qhd->khd/dot_general | solution.py:93
  715.9 12.2 %convert_reduce_fusion.5 = (f32[12,64]{1,0:T(8,128)S(1)}, bf16[12,64,1024]{2,1,0:T(8,128)(2,1)S(1)}) fusion(f32[12,64,1024]{2,1,0:T(8,128)S(1)} %fusion.28, bf16[512,12,64]{0,2,1:T(8,128)(2,1)S(1)} %bitcast.156, f32[12,512]{1,0:T(8,128)S(1)} %copy-done.73, f32[12,512,1024]{2,1,0:T(8,128)} %get-tuple-element.124, pred[512,1024]{1,0:T(8,128)(4,1)S(1)} %copy-done.29), kind=kOutput, calls=%fused_computation.162 | convolution fusion | flops 833617152 | bytes 31222784 | tf_op jit(solution)/shard_map/hqk,qhd->khd/dot_general | solution.py:93
  736.5 11.7 %fusion.24 = f32[12,64,1024]{2,1,0:T(8,128)S(1)} fusion(bf16[512,12,64]{0,2,1:T(8,128)(2,1)S(1)} %bitcast.154, f32[12,512]{1,0:T(8,128)S(1)} %copy-done.72, f32[12,512,1024]{2,1,0:T(8,128)} %get-tuple-element.118, pred[512,1024]{1,0:T(8,128)(4,1)S(1)} %copy-done.26), kind=kOutput, calls=%fused_computation.52 | convolution fusion | flops 830472192 | bytes 29646848 | tf_op jit(solution)/shard_map/hqk,qhd->khd/dot_general | solution.py:93
  748.3 12.0 %convert_reduce_fusion.4 = (f32[12,64]{1,0:T(8,128)S(1)}, bf16[12,64,1024]{2,1,0:T(8,128)(2,1)S(1)}) fusion(f32[12,64,1024]{2,1,0:T(8,128)S(1)} %fusion.24, bf16[512,12,64]{0,2,1:T(8,128)(2,1)S(1)} %bitcast.152, f32[12,512]{1,0:T(8,128)S(1)} %copy-done.70, f32[12,512,1024]{2,1,0:T(8,128)} %get-tuple-element.120, pred[512,1024]{1,0:T(8,128)(4,1)S(1)} %copy-done.24), kind=kOutput, calls=%fused_computation.161 | convolution fusion | flops 833617152 | bytes 31222784 | tf_op jit(solution)/shard_map/hqk,qhd->khd/dot_general | solution.py:93
  761.5 10.2 %convolution_add_fusion = f32[768,2304]{1,0:T(8,128)} fusion(f32[768,2304]{1,0:T(8,128)} %fusion.102, bf16[1024,768]{0,1:T(8,128)(2,1)S(1)} %bitcast.170, bf16[1024,768]{0,1:T(8,128)(2,1)S(1)} %bitcast.150, bf16[1024,768]{0,1:T(8,128)(2,1)S(1)} %bitcast.163, f32[1024]{0:T(1024)S(1)} %copy-done.94, f32[1024]{0:T(1024)S(1)} %copy-done.82, ...), kind=kOutput, calls=%fused_computation.98 | convolution fusion | flops 3644522496 | bytes 20463616 | tf_op jit(solution)/shard_map/rd,re->de/dot_general | solution.py:239
  789.4 59.6 %all-reduce.18 = (bf16[768]{0:T(1024)(128)(2,1)S(1)}, bf16[768]{0:T(1024)(128)(2,1)S(1)}, bf16[768]{0:T(1024)(128)(2,1)S(1)}, bf16[768]{0:T(1024)(128)(2,1)S(1)}...) all-reduce(f32[768]{0:T(1024)S(1)} %add.385, ...), channel_id=16, replica_groups=mesh['dp'=2,'fsdp'=16] {'fsdp'}, use_global_device_ids=true, to_apply=%region_29.30.clone | all-reduce | flops 9216 | bytes 55296
  866.5 10.3 %add_convert_fusion.4 = bf16[1024,768]{1,0:T(8,128)(2,1)} fusion(f32[1024,768]{1,0:T(8,128)S(1)} %copy-done.9, bf16[1024,3072]{1,0:T(8,128)(2,1)} %get-tuple-element.97, bf16[3072,768]{1,0:T(8,128)(2,1)} %all-gather.12.cloned.1.call-done, f32[768]{0:T(1024)S(1)} %convert_element_type.329), kind=kOutput, calls=%fused_computation.181 | convolution fusion | flops 4834197504 | bytes 15731712 | tf_op jit(solution)/shard_map/dot_general | solution.py:153
  906.1 16.3 %all-reduce.24.cloned.1.call-done = (bf16[48,768]{1,0:T(8,128)(2,1)}, bf16[48,3072]{1,0:T(8,128)(2,1)}, bf16[192,768]{1,0:T(8,128)(2,1)}) async-done(((bf16[48,768]{1,0:T(8,128)(2,1)}, bf16[48,3072]{1,0:T(8,128)(2,1)}, bf16[192,768]{1,0:T(8,128)(2,1)}), (bf16[48,768]{1,0:T(8,128)(2,1)}, bf16[48,3072]{1,0:T(8,128)(2,1)}, bf16[192,768]{1,0:T(8,128)(2,1)})) %all-reduce.24.cloned.1.call-update) | async-done | bytes 663568 | tf_op jit(solution)/shard_map/psum | solution.py:366
  (425 shorter events, 313.0 us)
Async XLA Ops:
  7.2 82.3 %copy-start.10 = (bf16[2048,768]{1,0:T(8,128)(2,1)S(1)}, bf16[2048,768]{1,0:T(8,128)(2,1)}, u32[]{:S(2)}) copy-start(bf16[2048,768]{1,0:T(8,128)(2,1)} %param.16) | copy-start | bytes 9437188
  7.2 86.3 %all-gather.6.cloned.1.call-start = ((), (), s32[]{:S(2)}) async-start(), calls=%async_computation.4 | async-start | bytes 3760128 | tf_op jit(solution)/shard_map/all_gather | solution.py:309
  7.9 285.6 %all-gather.8.cloned.1.call-start = ((), (), s32[]{:S(2)}) async-start(), calls=%async_computation.5 | async-start | bytes 1253376 | tf_op jit(solution)/shard_map/all_gather | solution.py:312
  8.7 295.9 %all-gather.10.cloned.1.call-start = ((), (), s32[]{:S(2)}) async-start(), calls=%async_computation.6 | async-start | bytes 5013504 | tf_op jit(solution)/shard_map/all_gather | solution.py:316
  9.4 306.1 %all-gather.12.cloned.1.call-start = ((), (), s32[]{:S(2)}) async-start(), calls=%async_computation.7 | async-start | bytes 5013504 | tf_op jit(solution)/shard_map/all_gather | solution.py:318
  10.0 873.0 %reduce-scatter.7.cloned.1.call-start = ((), (), s32[]{:S(2)}) async-start(), calls=%async_computation.9 | async-start | bytes 2506752 | tf_op jit(solution)/shard_map/reduce_scatter | solution.py:349
  85.2 19.0 %copy-start.102 = (f32[768]{0:T(1024)}, f32[768]{0:T(1024)S(1)}, u32[]{:S(2)}) copy-start(f32[768]{0:T(1024)S(1)} %convert_element_type.314) | copy-start | bytes 9220
  85.2 19.0 %copy-start.89 = (f32[768]{0:T(1024)}, f32[768]{0:T(1024)S(1)}, u32[]{:S(2)}) copy-start(f32[768]{0:T(1024)S(1)} %convert_element_type.313) | copy-start | bytes 9220
  104.3 151.5 %copy-start.7 = (bf16[1024,768]{0,1:T(8,128)(2,1)}, bf16[1024,768]{0,1:T(8,128)(2,1)S(1)}, u32[]{:S(2)}) copy-start(bf16[1024,768]{0,1:T(8,128)(2,1)S(1)} %copy.69) | copy-start | bytes 4718596
  118.1 64.6 %copy-start.6 = (bf16[1024,768]{0,1:T(8,128)(2,1)}, bf16[1024,768]{0,1:T(8,128)(2,1)S(1)}, u32[]{:S(2)}) copy-start(bf16[1024,768]{0,1:T(8,128)(2,1)S(1)} %copy.65) | copy-start | bytes 4718596
  144.7 24.9 %copy-start.18 = (bf16[1024,768]{0,1:T(8,128)(2,1)S(1)}, bf16[1024,768]{0,1:T(8,128)(2,1)}, u32[]{:S(2)}) copy-start(bf16[1024,768]{0,1:T(8,128)(2,1)} %copy.63) | copy-start | bytes 4718596
  157.0 16.2 %copy-start.3 = (f32[12,512,1024]{2,1,0:T(8,128)S(1)}, f32[12,512,1024]{2,1,0:T(8,128)}, u32[]{:S(2)}) copy-start(f32[12,512,1024]{2,1,0:T(8,128)} %get-tuple-element.122) | copy-start | bytes 75497472
  194.9 16.3 %copy-start.2 = (f32[12,512,1024]{2,1,0:T(8,128)S(1)}, f32[12,512,1024]{2,1,0:T(8,128)}, u32[]{:S(2)}) copy-start(f32[12,512,1024]{2,1,0:T(8,128)} %get-tuple-element.124) | copy-start | bytes 75497472
  194.9 16.4 %copy-start.27 = (pred[512,1024]{1,0:T(8,128)(4,1)S(1)}, pred[512,1024]{1,0:T(8,128)(4,1)}, u32[]{:S(2)}) copy-start(pred[512,1024]{1,0:T(8,128)(4,1)} %get-tuple-element.151) | copy-start | bytes 1572868
  219.8 24.5 %copy-start.20 = (bf16[1024,768]{0,1:T(8,128)(2,1)S(1)}, bf16[1024,768]{0,1:T(8,128)(2,1)}, u32[]{:S(2)}) copy-start(bf16[1024,768]{0,1:T(8,128)(2,1)} %copy.67) | copy-start | bytes 4718596
  255.9 24.4 %copy-start.63 = (bf16[512,12,64]{0,2,1:T(8,128)(2,1)S(1)}, bf16[512,12,64]{0,2,1:T(8,128)(2,1)}, u32[]{:S(2)}) copy-start(bf16[512,12,64]{0,2,1:T(8,128)(2,1)} %fusion.113) | copy-start | bytes 2359300
  267.9 16.1 %copy-start.1 = (f32[12,512,1024]{2,1,0:T(8,128)S(1)}, f32[12,512,1024]{2,1,0:T(8,128)}, u32[]{:S(2)}) copy-start(f32[12,512,1024]{2,1,0:T(8,128)} %get-tuple-element.120) | copy-start | bytes 75497472
  297.5 143.9 %copy-start.8 = (f32[1024,768]{1,0:T(8,128)}, f32[1024,768]{1,0:T(8,128)S(1)}, u32[]{:S(2)}) copy-start(f32[1024,768]{1,0:T(8,128)S(1)} %get-tuple-element.126) | copy-start | bytes 9437188
  315.6 20.3 %slice-start.7 = ((s8[12582912]{0:T(1024)(128)(4,1)}), s8[4194304]{0:T(1024)(128)(4,1)S(1)}, s32[]{:S(2)}) async-start(s8[12582912]{0:T(1024)(128)(4,1)} %bitcast.172), calls=%async_computation.20 | async-start | bytes 8388608
  315.6 20.3 %slice-start.8 = ((s8[12582912]{0:T(1024)(128)(4,1)}), s8[4194304]{0:T(1024)(128)(4,1)S(1)}, s32[]{:S(2)}) async-start(s8[12582912]{0:T(1024)(128)(4,1)} %bitcast.172), calls=%async_computation.21 | async-start | bytes 8388608
  335.8 61.7 %copy-start.48 = (bf16[2048,768]{1,0:T(8,128)(2,1)S(1)}, bf16[2048,768]{1,0:T(8,128)(2,1)}, u32[]{:S(2)}) copy-start(bf16[2048,768]{1,0:T(8,128)(2,1)} %param.17) | copy-start | bytes 9437188
  433.4 451.3 %reduce-scatter.9.cloned.1.call-start = ((), (), s32[]{:S(2)}) async-start(), calls=%async_computation.10 | async-start | bytes 10027008 | tf_op jit(solution)/shard_map/reduce_scatter | solution.py:353
  458.4 428.1 %reduce-scatter.11.cloned.1.call-start = ((), (), s32[]{:S(2)}) async-start(), calls=%async_computation.11 | async-start | bytes 10027008 | tf_op jit(solution)/shard_map/reduce_scatter | solution.py:355
  572.0 321.9 %reduce-scatter.5.cloned.1.call-start = ((), (), s32[]{:S(2)}) async-start(), calls=%async_computation.8 | async-start | bytes 7520256 | tf_op jit(solution)/shard_map/reduce_scatter | solution.py:346
  595.5 22.1 %copy-start.30 = (pred[512,1024]{1,0:T(8,128)(4,1)S(1)}, pred[512,1024]{1,0:T(8,128)(4,1)}, u32[]{:S(2)}) copy-start(pred[512,1024]{1,0:T(8,128)(4,1)} %get-tuple-element.150) | copy-start | bytes 1572868
  595.5 22.1 %copy-start.57 = (bf16[512,768]{0,1:T(8,128)(2,1)S(1)}, bf16[512,768]{0,1:T(8,128)(2,1)}, u32[]{:S(2)}) copy-start(bf16[512,768]{0,1:T(8,128)(2,1)} %get-tuple-element.90) | copy-start | bytes 2359300
  595.5 22.1 %copy-start.74 = (f32[12,512]{1,0:T(8,128)S(1)}, f32[12,512]{1,0:T(8,128)}, u32[]{:S(2)}) copy-start(f32[12,512]{1,0:T(8,128)} %log_add_fusion.2) | copy-start | bytes 73732
  640.5 19.0 %copy-start.46 = (bf16[512,12,64]{0,2,1:T(8,128)(2,1)S(1)}, bf16[512,12,64]{0,2,1:T(8,128)(2,1)}, u32[]{:S(2)}) copy-start(bf16[512,12,64]{0,2,1:T(8,128)(2,1)} %multiply_bitcast_fusion.1) | copy-start | bytes 2359300
  640.5 19.0 %copy-start.47 = (bf16[512,12,64]{0,2,1:T(8,128)(2,1)S(1)}, bf16[512,12,64]{0,2,1:T(8,128)(2,1)}, u32[]{:S(2)}) copy-start(bf16[512,12,64]{0,2,1:T(8,128)(2,1)} %multiply_bitcast_fusion) | copy-start | bytes 2359300
  771.8 150.6 %all-reduce.24.cloned.1.call-start = ((), (), s32[]{:S(2)}) async-start(), calls=%async_computation.12 | async-start | bytes 1327104 | tf_op jit(solution)/shard_map/psum | solution.py:366
  859.3 17.4 %slice-start.5 = ((s8[4718592]{0:T(1024)(128)(4,1)}), s8[4194304]{0:T(1024)(128)(4,1)S(1)}, s32[]{:S(2)}) async-start(s8[4718592]{0:T(1024)(128)(4,1)} %bitcast.166), calls=%async_computation.18 | async-start | bytes 8388608
  859.4 17.4 %slice-start.10 = ((s8[6291456]{0:T(1024)(128)(4,1)}), s8[4194304]{0:T(1024)(128)(4,1)S(1)}, s32[]{:S(2)}) async-start(s8[6291456]{0:T(1024)(128)(4,1)} %bitcast.174), calls=%async_computation.23 | async-start | bytes 8388608
  (102 other events, 770.1 us)
Sparse Core Ops, SparseCore 0:
  10.3 49.9 all-gather.5
  62.6 37.2 all-gather.7
  102.2 52.1 all-gather.9
  156.5 51.7 all-gather.11
  433.5 60.1 reduce-scatter.6
  498.2 110.3 reduce-scatter.8
  612.6 111.1 reduce-scatter.10
  771.9 88.1 reduce-scatter.4
  888.5 33.8 all-reduce.23
